TPU v7x, 32 devices: a whole 2x2x4 slice. The times are simulated.
32 devices in a mesh: dp: 4 (over z), rows: 4 (over y, core), cols: 2 (over x).
Axes of the slice: x: 2, y: 2, z: 4, core: 2. Of those that a mesh axis runs over, the one named last changes fastest.
Arguments:
- hidden_in: bfloat16 [3072, 1536], P(('dp', 'cols'), 'rows'), may hold values from -7 to 7
- attn_gain: float32 [2, 1536], P(None, 'rows'), may hold values from 0.1 to 1.9
- w_qkv: bfloat16 [2, 1536, 2048], P(None, 'rows', 'cols'), may hold values from -0.15625 to 0.15625
- b_qkv: float32 [2, 2048], P(None, 'cols'), may hold values from -2 to 2
- w_out: bfloat16 [2, 1536, 1536], P(None, 'cols', 'rows'), may hold values from -0.3125 to 0.3125
- mlp_gain: float32 [2, 1536], P(None, 'rows'), may hold values from 0.1 to 1.9
- w_gate: bfloat16 [2, 1536, 8960], P(None, 'rows', 'cols'), may hold values from -0.15625 to 0.15625
- w_up: bfloat16 [2, 1536, 8960], P(None, 'rows', 'cols'), may hold values from -0.15625 to 0.15625
- w_down: bfloat16 [2, 8960, 1536], P(None, 'cols', 'rows'), may hold values from -0.0625 to 0.0625
- out_grad: bfloat16 [3072, 1536], P(('dp', 'cols'), 'rows'), may hold values from -6 to 6
Outputs:
- hidden_out: bfloat16 [3072, 1536], P(('dp', 'cols'), 'rows')
- in_grad: float32 [3072, 1536], P(('dp', 'cols'), 'rows')
- attn_gain_grad: float32 [2, 1536], P(None, 'rows')
- w_qkv_grad: float32 [2, 1536, 2048], P(None, 'rows', 'cols')
- b_qkv_grad: float32 [2, 2048], P(None, 'cols')
- w_out_grad: float32 [2, 1536, 1536], P(None, 'cols', 'rows')
- mlp_gain_grad: float32 [2, 1536], P(None, 'rows')
- w_gate_grad: float32 [2, 1536, 8960], P(None, 'rows', 'cols')
- w_up_grad: float32 [2, 1536, 8960], P(None, 'rows', 'cols')
- w_down_grad: float32 [2, 8960, 1536], P(None, 'cols', 'rows')
All inputs are finite; a program needn't handle non-finite values.
Results may differ from a plain program's by a relative error of at most 0.025.
Values may be sent and summed in bfloat16 or wider, within the bound.
No kernel may reach another device: no remote copies, remote signals or barrier semaphores. Data moves between devices by JAX's collectives and lax.ppermute only.
A program may use at most 320 MiB of HBM per device.

v0:
```python
import jax
import jax.numpy as jnp
from jax import lax
from jax.sharding import PartitionSpec as P

D = 1536
HEADS = 12
KV_HEADS = 2
HEAD_DIM = 128
SEQ = 192
LAYERS = 2
QKV = 2048
eps = 1e-06
theta = 1000000.0
masked = -1e30


def rotate_half(values):
    half_dim = values.shape[-1] // 2
    return jnp.concatenate([-values[..., half_dim:], values[..., :half_dim]], axis=-1)


def rope_tables():
    frequency = theta ** (-jnp.arange(0, HEAD_DIM, 2, dtype=jnp.float32) / HEAD_DIM)
    angles = jnp.arange(SEQ, dtype=jnp.float32)[:, None] * frequency[None, :]
    angles = jnp.concatenate([angles, angles], axis=-1)
    return (jnp.cos(angles), jnp.sin(angles))


def causal_scores(query_round, key_round):
    raw_scores = jnp.einsum(
        "sikgd,sjkd->skgij", query_round, key_round, preferred_element_type=jnp.float32
    ) * HEAD_DIM ** (-0.5)
    position = jnp.arange(SEQ)
    return jnp.where(position[:, None] >= position[None, :], raw_scores, masked)


def attention_forward(qkv_rows, kv_count, group_size):
    blocks = qkv_rows.reshape(-1, SEQ, kv_count, group_size + 2, HEAD_DIM)
    cosine, sine_table = rope_tables()
    query = blocks[:, :, :, :group_size]
    key_part = blocks[:, :, :, group_size]
    value_part = blocks[:, :, :, group_size + 1]
    query = (
        query * cosine[None, :, None, None, :]
        + rotate_half(query) * sine_table[None, :, None, None, :]
    )
    key_part = (
        key_part * cosine[None, :, None, :] + rotate_half(key_part) * sine_table[None, :, None, :]
    )
    query_round = query.astype(jnp.bfloat16)
    key_round = key_part.astype(jnp.bfloat16)
    value_round = value_part.astype(jnp.bfloat16)
    scores = causal_scores(query_round, key_round)
    highest = jnp.max(scores, axis=-1, keepdims=True)
    log_total = highest + jnp.log(jnp.sum(jnp.exp(scores - highest), axis=-1, keepdims=True))
    weights_round = jnp.exp(scores - log_total).astype(jnp.bfloat16)
    attended = jnp.einsum(
        "skgij,sjkd->sikgd", weights_round, value_round, preferred_element_type=jnp.float32
    )
    attended = attended.astype(jnp.bfloat16).reshape(qkv_rows.shape[0], -1)
    return (attended, (query_round, key_round, value_round, log_total))


def attention_backward(grad_attended, attn_kept, kv_count, group_size):
    query_round, key_round, value_round, log_total = attn_kept
    grad_round = grad_attended.astype(jnp.bfloat16).reshape(-1, SEQ, kv_count, group_size, HEAD_DIM)
    scores = causal_scores(query_round, key_round)
    prob_full = jnp.exp(scores - log_total)
    weights_round = prob_full.astype(jnp.bfloat16)
    grad_value = jnp.einsum(
        "skgij,sikgd->sjkd", weights_round, grad_round, preferred_element_type=jnp.float32
    )
    grad_prob = jnp.einsum(
        "sikgd,sjkd->skgij", grad_round, value_round, preferred_element_type=jnp.float32
    )
    grad_scores = (
        prob_full
        * (grad_prob - jnp.sum(prob_full * grad_prob, axis=-1, keepdims=True))
        * HEAD_DIM ** (-0.5)
    )
    grad_scores = grad_scores.astype(jnp.bfloat16)
    grad_query = jnp.einsum(
        "skgij,sjkd->sikgd", grad_scores, key_round, preferred_element_type=jnp.float32
    )
    grad_key = jnp.einsum(
        "skgij,sikgd->sjkd", grad_scores, query_round, preferred_element_type=jnp.float32
    )
    cosine, sine_table = rope_tables()
    grad_query = (
        grad_query * cosine[None, :, None, None, :]
        - rotate_half(grad_query) * sine_table[None, :, None, None, :]
    )
    grad_key = (
        grad_key * cosine[None, :, None, :] - rotate_half(grad_key) * sine_table[None, :, None, :]
    )
    joined = jnp.concatenate(
        [grad_query, grad_key[:, :, :, None], grad_value[:, :, :, None]], axis=3
    )
    return joined.reshape(grad_attended.shape[0], -1)


def norm_forward(resid, gain_row):
    squares = jnp.sum(resid * resid, axis=1)
    totals = lax.psum(squares, "rows")
    scale_row = lax.rsqrt(totals / D + eps)
    normed = (resid * scale_row[:, None] * gain_row[None, :]).astype(jnp.bfloat16)
    return (normed, scale_row)


def norm_backward(grad_normed, resid, scale_row, gain_row):
    scaled = grad_normed * gain_row[None, :]
    inner = lax.psum(jnp.sum(scaled * resid, axis=1), "rows")
    gain_grad = jnp.sum(grad_normed * resid * scale_row[:, None], axis=0)
    grad_resid = (
        scale_row[:, None] * scaled
        - resid * (scale_row * scale_row * scale_row * inner / D)[:, None]
    )
    return (grad_resid, gain_grad)


def gather_cols(values):
    return lax.all_gather(values, "cols", axis=0, tiled=True)


def gather_rows(values):
    return lax.all_gather(values, "rows", axis=0, tiled=True)


def widen(gathered, weight):
    per_device = gathered.shape[0] // lax.axis_size("rows")

    def partial_term(first_row, length_rows):
        return jnp.dot(gathered, weight, preferred_element_type=jnp.float32)

    return lax.psum_scatter(
        partial_term(jnp.int32(0), lax.axis_size("rows") * per_device),
        "rows",
        scatter_dimension=0,
        tiled=True,
    )


def narrow(gathered, weight):
    per_device = gathered.shape[0] // lax.axis_size("cols")

    def partial_term(first_row, length_rows):
        return jnp.dot(gathered, weight, preferred_element_type=jnp.float32)

    return lax.psum_scatter(
        partial_term(jnp.int32(0), per_device * lax.axis_size("cols")).astype(jnp.bfloat16),
        "cols",
        scatter_dimension=0,
        tiled=True,
    ).astype(jnp.float32)


def back_narrow(grad_resid, weight):
    grad_round = grad_resid.astype(jnp.bfloat16)
    gathered = lax.all_gather(grad_round, "cols", axis=0, tiled=True)
    per_device = gathered.shape[0] // lax.axis_size("rows")

    def partial_term(first_row, length_rows):
        return lax.dot_general(
            gathered, weight, (((1,), (1,)), ((), ())), preferred_element_type=jnp.float32
        )

    return (
        lax.psum_scatter(
            partial_term(jnp.int32(0), per_device * lax.axis_size("rows")).astype(jnp.bfloat16),
            "rows",
            scatter_dimension=0,
            tiled=True,
        ).astype(jnp.float32),
        gathered,
    )


def back_widen(grad_round, weight):
    gathered = lax.all_gather(grad_round, "rows", axis=0, tiled=True)
    per_device = gathered.shape[0] // lax.axis_size("cols")

    def partial_term(first_row, length_rows):
        return lax.dot_general(
            gathered, weight, (((1,), (1,)), ((), ())), preferred_element_type=jnp.float32
        )

    return (
        lax.psum_scatter(
            partial_term(jnp.int32(0), per_device * lax.axis_size("cols")).astype(jnp.bfloat16),
            "cols",
            scatter_dimension=0,
            tiled=True,
        ).astype(jnp.float32),
        gathered,
    )


def weight_grad(left_rows, right_rows):
    return lax.dot_general(
        left_rows, right_rows, (((0,), (0,)), ((), ())), preferred_element_type=jnp.float32
    )


def spread(first_grad, second_grad, third_grad, fourth_grad, fifth_grad):
    summed = (
        lax.psum_scatter(
            first_grad.astype(jnp.bfloat16), "dp", scatter_dimension=1, tiled=True
        ).astype(jnp.float32),
        lax.psum_scatter(
            second_grad.astype(jnp.bfloat16), "dp", scatter_dimension=1, tiled=True
        ).astype(jnp.float32),
        lax.psum_scatter(
            third_grad.astype(jnp.bfloat16), "dp", scatter_dimension=1, tiled=True
        ).astype(jnp.float32),
        lax.psum_scatter(
            fourth_grad.astype(jnp.bfloat16), "dp", scatter_dimension=1, tiled=True
        ).astype(jnp.float32),
        lax.psum_scatter(
            fifth_grad.astype(jnp.bfloat16), "dp", scatter_dimension=1, tiled=True
        ).astype(jnp.float32),
    )
    return (
        lax.all_gather(summed[0].astype(jnp.bfloat16), "dp", axis=1, tiled=True).astype(
            jnp.float32
        ),
        lax.all_gather(summed[1].astype(jnp.bfloat16), "dp", axis=1, tiled=True).astype(
            jnp.float32
        ),
        lax.all_gather(summed[2].astype(jnp.bfloat16), "dp", axis=1, tiled=True).astype(
            jnp.float32
        ),
        lax.all_gather(summed[3].astype(jnp.bfloat16), "dp", axis=1, tiled=True).astype(
            jnp.float32
        ),
        lax.all_gather(summed[4].astype(jnp.bfloat16), "dp", axis=1, tiled=True).astype(
            jnp.float32
        ),
    )


def body(hidden_in, attn_gain, w_qkv, b_qkv, w_out, mlp_gain, w_gate, w_up, w_down, out_grad):
    kv_count = KV_HEADS // lax.axis_size("cols")
    group_size = HEADS // KV_HEADS
    hidden_units = w_gate.shape[2]
    resid = hidden_in.astype(jnp.float32)
    saved = []
    for which_layer in range(LAYERS):
        normed_attn, scale_attn = norm_forward(resid, attn_gain[which_layer])
        gathered_attn = gather_cols(normed_attn)
        qkv_rows = widen(gathered_attn, w_qkv[which_layer]) + b_qkv[which_layer][None, :]
        attended, attn_kept = attention_forward(qkv_rows, kv_count, group_size)
        gathered_heads = gather_rows(attended)
        middle = resid + narrow(gathered_heads, w_out[which_layer])
        normed_mlp, scale_mlp = norm_forward(middle, mlp_gain[which_layer])
        gathered_mlp = gather_cols(normed_mlp)
        joined = jnp.concatenate([w_gate[which_layer], w_up[which_layer]], axis=1)
        both_proj = widen(gathered_mlp, joined)
        gate_proj = both_proj[:, :hidden_units]
        up_proj = both_proj[:, hidden_units:]
        activated = (jax.nn.silu(gate_proj) * up_proj).astype(jnp.bfloat16)
        gathered_units = gather_rows(activated)
        store = (gathered_attn, gathered_heads, gathered_mlp, gathered_units)
        saved.append((resid, scale_attn, attn_kept, middle, scale_mlp, gate_proj, up_proj, store))
        resid = middle + narrow(gathered_units, w_down[which_layer])
    hidden_out = resid.astype(jnp.bfloat16)
    grad_resid = out_grad.astype(jnp.float32)
    layer_grads = [None] * LAYERS
    attn_gain_parts = [None] * LAYERS
    mlp_gain_parts = [None] * LAYERS
    bias_parts = [None] * LAYERS
    for which_layer in reversed(range(LAYERS)):
        resid, scale_attn, attn_kept, middle, scale_mlp, gate_proj, up_proj, store = saved[
            which_layer
        ]
        rows_attn, rows_heads, rows_mlp, rows_units = store
        grad_units, down_gathered = back_narrow(grad_resid, w_down[which_layer])
        down_grad = weight_grad(rows_units, down_gathered)
        sigmoid_gate = jax.nn.sigmoid(gate_proj)
        grad_gate = grad_units * up_proj * sigmoid_gate * (1.0 + gate_proj * (1.0 - sigmoid_gate))
        grad_up = grad_units * gate_proj * sigmoid_gate
        grad_both = jnp.concatenate(
            [grad_gate.astype(jnp.bfloat16), grad_up.astype(jnp.bfloat16)], axis=1
        )
        joined = jnp.concatenate([w_gate[which_layer], w_up[which_layer]], axis=1)
        grad_normed_mlp, both_gathered = back_widen(grad_both, joined)
        both_grad = weight_grad(rows_mlp, both_gathered)
        grad_inner, mlp_gain_part = norm_backward(
            grad_normed_mlp, middle, scale_mlp, mlp_gain[which_layer]
        )
        grad_middle = grad_resid + grad_inner
        grad_heads, heads_gathered = back_narrow(grad_middle, w_out[which_layer])
        out_weight_grad = weight_grad(rows_heads, heads_gathered)
        grad_qkv = attention_backward(grad_heads, attn_kept, kv_count, group_size)
        bias_part = jnp.sum(grad_qkv, axis=0)
        grad_normed_attn, qkv_gathered = back_widen(
            grad_qkv.astype(jnp.bfloat16), w_qkv[which_layer]
        )
        qkv_weight_grad = weight_grad(rows_attn, qkv_gathered)
        grad_first, attn_gain_part = norm_backward(
            grad_normed_attn, resid, scale_attn, attn_gain[which_layer]
        )
        grad_resid = grad_middle + grad_first
        attn_gain_parts[which_layer] = attn_gain_part
        mlp_gain_parts[which_layer] = mlp_gain_part
        bias_parts[which_layer] = bias_part
        grads_now = (
            qkv_weight_grad,
            out_weight_grad,
            both_grad[:, :hidden_units],
            both_grad[:, hidden_units:],
            down_grad,
        )
        layer_grads[which_layer] = grads_now
    stacked = [
        jnp.stack([layer_grads[which_layer][member] for which_layer in range(LAYERS)])
        for member in range(5)
    ]
    merged = spread(stacked[0], stacked[1], stacked[2], stacked[3], stacked[4])
    row_width = attn_gain.shape[1]
    col_width = b_qkv.shape[1]
    row_place = lax.axis_index("rows") * row_width
    col_place = lax.axis_index("cols") * col_width
    attn_full = lax.dynamic_update_slice(
        jnp.zeros((LAYERS, D), jnp.float32), jnp.stack(attn_gain_parts), (0, row_place)
    )
    mlp_full = lax.dynamic_update_slice(
        jnp.zeros((LAYERS, D), jnp.float32), jnp.stack(mlp_gain_parts), (0, row_place)
    )
    bias_full = lax.dynamic_update_slice(
        jnp.zeros((LAYERS, QKV), jnp.float32), jnp.stack(bias_parts), (0, col_place)
    )
    totals = lax.psum((attn_full, mlp_full, bias_full), ("dp", "rows", "cols"))
    attn_gain_grad = lax.dynamic_slice_in_dim(totals[0], row_place, row_width, 1)
    mlp_gain_grad = lax.dynamic_slice_in_dim(totals[1], row_place, row_width, 1)
    bias_grad = lax.dynamic_slice_in_dim(totals[2], col_place, col_width, 1)
    return (
        hidden_out,
        grad_resid,
        attn_gain_grad,
        merged[0],
        bias_grad,
        merged[1],
        mlp_gain_grad,
        merged[2],
        merged[3],
        merged[4],
    )


def solution(mesh):
    in_specs = (
        P(("dp", "cols"), "rows"),
        P(None, "rows"),
        P(None, "rows", "cols"),
        P(None, "cols"),
        P(None, "cols", "rows"),
        P(None, "rows"),
        P(None, "rows", "cols"),
        P(None, "rows", "cols"),
        P(None, "cols", "rows"),
        P(("dp", "cols"), "rows"),
    )
    out_specs = (
        P(("dp", "cols"), "rows"),
        P(("dp", "cols"), "rows"),
        P(None, "rows"),
        P(None, "rows", "cols"),
        P(None, "cols"),
        P(None, "cols", "rows"),
        P(None, "rows"),
        P(None, "rows", "cols"),
        P(None, "rows", "cols"),
        P(None, "cols", "rows"),
    )
    return jax.shard_map(body, mesh=mesh, in_specs=in_specs, out_specs=out_specs, check_vma=False)
```

profile of v0, /device:TPU:0, one launch (start us, length us, event | category | flops | bytes accessed | tf_op | source)
XLA Modules:
  0.0 2279.8 jit_solution(14332408452359226671)
XLA Ops:
  32.6 38.2 %reduce-scatter.22.cloned.1.call-done = f32[192,1024]{1,0:T(8,128)} async-done(((f32[768,1024]{1,0:T(8,128)}), f32[192,1024]{1,0:T(8,128)}) %reduce-scatter.22.cloned.1.call-update) | async-done | bytes 786448 | tf_op jit(solution)/shard_map/reduce_scatter | solution.py:136
  77.2 16.9 all-gather.14.cloned.1.call-done
  97.0 10.2 slice_bitcast_fusion.4
  121.1 8.7 all_gather.65
  130.7 15.9 fusion.5
  146.7 197.8 %reduce-scatter.26.cloned.1.call-done = f32[192,8960]{1,0:T(8,128)} async-done(((f32[768,8960]{1,0:T(8,128)}), f32[192,8960]{1,0:T(8,128)}) %reduce-scatter.26.cloned.1.call-update) | async-done | bytes 6881296 | tf_op jit(solution)/shard_map/reduce_scatter | solution.py:136
  350.2 49.3 %all-gather.16.cloned.1.call-done = bf16[768,4480]{1,0:T(8,128)(2,1)} async-done(((bf16[192,4480]{1,0:T(8,128)(2,1)}), bf16[768,4480]{1,0:T(8,128)(2,1)}) %all-gather.16.cloned.1.call-update) | async-done | bytes 6881296 | tf_op jit(solution)/shard_map/all_gather | solution.py:127
  408.1 15.5 reduce-scatter.28.cloned.1.call-done
  431.3 8.7 all_gather.67
  444.1 38.0 %reduce-scatter.30.cloned.1.call-done = f32[192,1024]{1,0:T(8,128)} async-done(((f32[768,1024]{1,0:T(8,128)}), f32[192,1024]{1,0:T(8,128)}) %reduce-scatter.30.cloned.1.call-update) | async-done | bytes 786448 | tf_op jit(solution)/shard_map/reduce_scatter | solution.py:136
  487.9 17.5 all-gather.18.cloned.1.call-done
  508.5 13.0 all_gather.71
  540.2 10.2 all_gather.69
  551.2 17.1 fusion.3
  568.4 25.3 %reduce-scatter.38.cloned.1.call-done = bf16[192,4480]{1,0:T(8,128)(2,1)} async-done(((bf16[768,4480]{1,0:T(8,128)(2,1)}), bf16[192,4480]{1,0:T(8,128)(2,1)}) %reduce-scatter.38.cloned.1.call-update) | async-done | bytes 1720336 | tf_op jit(solution)/shard_map/reduce_scatter | solution.py:169
  593.7 200.3 %reduce-scatter.34.cloned.1.call-done = f32[192,8960]{1,0:T(8,128)} async-done(((f32[768,8960]{1,0:T(8,128)}), f32[192,8960]{1,0:T(8,128)}) %reduce-scatter.34.cloned.1.call-update) | async-done | bytes 6881296 | tf_op jit(solution)/shard_map/reduce_scatter | solution.py:136
  801.5 88.9 %all-gather.22.cloned.1.call-done = bf16[768,8960]{1,0:T(8,128)(2,1)} async-done(((bf16[192,8960]{1,0:T(8,128)(2,1)}), bf16[768,8960]{1,0:T(8,128)(2,1)}) %all-gather.22.cloned.1.call-update) | async-done | bytes 13762576 | tf_op jit(solution)/shard_map/all_gather | solution.py:180
  890.4 13.2 fusion.35
  903.7 15.5 reduce-scatter.40.cloned.1.call-done
  930.8 8.7 all_gather.73
  943.3 25.7 %reduce-scatter.42.cloned.1.call-done = bf16[192,768]{1,0:T(8,128)(2,1)} async-done(((bf16[768,768]{1,0:T(8,128)(2,1)}), bf16[192,768]{1,0:T(8,128)(2,1)}) %reduce-scatter.42.cloned.1.call-update) | async-done | bytes 294928 | tf_op jit(solution)/shard_map/reduce_scatter | solution.py:169
  974.8 19.2 all-gather.24.cloned.1.call-done
  997.7 47.9 %all-gather.20.cloned.1.call-done = bf16[768,4480]{1,0:T(8,128)(2,1)} async-done(((bf16[192,4480]{1,0:T(8,128)(2,1)}), bf16[768,4480]{1,0:T(8,128)(2,1)}) %all-gather.20.cloned.1.call-update) | async-done | bytes 6881296 | tf_op jit(solution)/shard_map/all_gather | solution.py:127
  1054.2 9.5 reduce-scatter.44.cloned.1.call-done
  1072.5 9.3 reduce-scatter.36.cloned.1.call-done
  1084.1 9.2 all_gather.75
  1102.0 63.0 %reduce-scatter.46.cloned.1.call-done = bf16[192,4480]{1,0:T(8,128)(2,1)} async-done(((bf16[768,4480]{1,0:T(8,128)(2,1)}), bf16[192,4480]{1,0:T(8,128)(2,1)}) %reduce-scatter.46.cloned.1.call-update) | async-done | bytes 1720336 | tf_op jit(solution)/shard_map/reduce_scatter | solution.py:169
  1171.4 88.9 %all-gather.26.cloned.1.call-done = bf16[768,8960]{1,0:T(8,128)(2,1)} async-done(((bf16[192,8960]{1,0:T(8,128)(2,1)}), bf16[768,8960]{1,0:T(8,128)(2,1)}) %all-gather.26.cloned.1.call-update) | async-done | bytes 13762576 | tf_op jit(solution)/shard_map/all_gather | solution.py:180
  1260.2 13.1 fusion.34
  1273.4 15.4 reduce-scatter.48.cloned.1.call-done
  1298.2 8.7 all_gather.77
  1311.1 25.3 %reduce-scatter.50.cloned.1.call-done = bf16[192,768]{1,0:T(8,128)(2,1)} async-done(((bf16[768,768]{1,0:T(8,128)(2,1)}), bf16[192,768]{1,0:T(8,128)(2,1)}) %reduce-scatter.50.cloned.1.call-update) | async-done | bytes 294928 | tf_op jit(solution)/shard_map/reduce_scatter | solution.py:169
  1365.6 11.7 convolution_convert_fusion
  1386.1 11.1 convolution_convert_fusion.1
  1410.7 73.6 %reduce-scatter.62.cloned.1.call-done = bf16[2,1120,384]{2,1,0:T(8,128)(2,1)} async-done(((bf16[2,4480,384]{2,1,0:T(8,128)(2,1)}), bf16[2,1120,384]{2,1,0:T(8,128)(2,1)}) %reduce-scatter.62.cloned.1.call-update) | async-done | bytes 1720336 | tf_op jit(solution)/shard_map/reduce_scatter | solution.py:219
  1484.4 32.7 %reduce-scatter.56.cloned.1.call-done = bf16[2,192,384]{2,1,0:T(8,128)(2,1)} async-done(((bf16[2,768,384]{2,1,0:T(8,128)(2,1)}), bf16[2,192,384]{2,1,0:T(8,128)(2,1)}) %reduce-scatter.56.cloned.1.call-update) | async-done | bytes 294928 | tf_op jit(solution)/shard_map/reduce_scatter | solution.py:210
  1520.8 33.1 %reduce-scatter.54.cloned.1.call-done = bf16[2,96,1024]{2,1,0:T(8,128)(2,1)} async-done(((bf16[2,384,1024]{2,1,0:T(8,128)(2,1)}), bf16[2,96,1024]{2,1,0:T(8,128)(2,1)}) %reduce-scatter.54.cloned.1.call-update) | async-done | bytes 393232 | tf_op jit(solution)/shard_map/reduce_scatter | solution.py:207
  1554.0 121.9 %reduce-scatter.58.cloned.1.call-done = bf16[2,96,4480]{2,1,0:T(8,128)(2,1)} async-done(((bf16[2,384,4480]{2,1,0:T(8,128)(2,1)}), bf16[2,96,4480]{2,1,0:T(8,128)(2,1)}) %reduce-scatter.58.cloned.1.call-update) | async-done | bytes 1720336 | tf_op jit(solution)/shard_map/reduce_scatter | solution.py:213
  1676.1 123.5 %reduce-scatter.60.cloned.1.call-done = bf16[2,96,4480]{2,1,0:T(8,128)(2,1)} async-done(((bf16[2,384,4480]{2,1,0:T(8,128)(2,1)}), bf16[2,96,4480]{2,1,0:T(8,128)(2,1)}) %reduce-scatter.60.cloned.1.call-update) | async-done | bytes 1720336 | tf_op jit(solution)/shard_map/reduce_scatter | solution.py:216
  1799.8 126.9 %all-gather.38.cloned.1.call-done = bf16[2,4480,384]{2,1,0:T(8,128)(2,1)} async-done(((bf16[2,1120,384]{2,1,0:T(8,128)(2,1)}), bf16[2,4480,384]{2,1,0:T(8,128)(2,1)}) %all-gather.38.cloned.1.call-update) | async-done | bytes 6881296 | tf_op jit(solution)/shard_map/all_gather | solution.py:236
  1926.7 9.0 convert_element_type.303
  1935.9 20.7 all-gather.32.cloned.1.call-done
  1959.4 14.6 reduce-scatter.52.cloned.1.call-done
  1981.7 41.7 %all-reduce = (f32[2,1536]{1,0:T(2,128)S(1)}, f32[2,2048]{1,0:T(2,128)S(1)}, f32[2,1536]{1,0:T(2,128)S(1)}) all-reduce(f32[2,1536]{1,0:T(2,128)S(1)} %maximum_dynamic-update-slice_fusion.1, f32[2,2048]{1,0:T(2,128)S(1)} %maximum_dynamic-update-slice_fusion, ...), channel_id=1, replica_groups=mesh['dp'=4,'rows'=4,'cols'=2] {'dp','rows','cols'}, use_global_device_ids=true, to_apply=%region_40.41 | all-reduce | flops 10240 | bytes 81920 | tf_op jit(solution)/shard_map/psum | solution.py:333
  2030.9 108.1 %all-gather.34.cloned.1.call-done = bf16[2,384,4480]{2,1,0:T(8,128)(2,1)} async-done(((bf16[2,96,4480]{2,1,0:T(8,128)(2,1)}), bf16[2,384,4480]{2,1,0:T(8,128)(2,1)}) %all-gather.34.cloned.1.call-update) | async-done | bytes 6881296 | tf_op jit(solution)/shard_map/all_gather | solution.py:230
  2139.0 9.6 convert_element_type.301
  2148.6 115.2 %all-gather.36.cloned.1.call-done = bf16[2,384,4480]{2,1,0:T(8,128)(2,1)} async-done(((bf16[2,96,4480]{2,1,0:T(8,128)(2,1)}), bf16[2,384,4480]{2,1,0:T(8,128)(2,1)}) %all-gather.36.cloned.1.call-update) | async-done | bytes 6881296 | tf_op jit(solution)/shard_map/all_gather | solution.py:233
  2263.7 9.0 convert_element_type.302
  (389 shorter events, 256.9 us)
Async XLA Ops:
  7.2 63.6 %reduce-scatter.22.cloned.1.call-start = ((), (), s32[]{:S(2)}) async-start(), calls=%async_computation.21 | async-start | bytes 3932160 | tf_op jit(solution)/shard_map/reduce_scatter | solution.py:136
  8.0 423.2 %copy-start.64 = (f32[384]{0:T(512)}, f32[384]{0:T(512)S(1)}, u32[]{:S(2)}) copy-start(f32[384]{0:T(512)S(1)} %get-tuple-element.18) | copy-start | bytes 4612
  31.4 62.7 %all-gather.14.cloned.1.call-start = ((), (), s32[]{:S(2)}) async-start(), calls=%async_computation.22 | async-start | bytes 1474560 | tf_op jit(solution)/shard_map/all_gather | solution.py:127
  32.6 452.2 %copy-start.16 = (f32[192,128]{1,0:T(8,128)}, f32[192,128]{1,0:T(8,128)S(1)}, u32[]{:S(2)}) copy-start(f32[192,128]{1,0:T(8,128)S(1)} %get-tuple-element.59) | copy-start | bytes 294916
  32.6 452.2 %copy-start.19 = (f32[192,128]{1,0:T(8,128)}, f32[192,128]{1,0:T(8,128)S(1)}, u32[]{:S(2)}) copy-start(f32[192,128]{1,0:T(8,128)S(1)} %get-tuple-element.60) | copy-start | bytes 294916
  76.5 36.0 %reduce-scatter.24.cloned.1.call-start = ((), (), s32[]{:S(2)}) async-start(), calls=%async_computation.23 | async-start | bytes 884736 | tf_op jit(solution)/shard_map/reduce_scatter | solution.py:150
  97.0 247.5 %reduce-scatter.26.cloned.1.call-start = ((), (), s32[]{:S(2)}) async-start(), calls=%async_computation.24 | async-start | bytes 34406400 | tf_op jit(solution)/shard_map/reduce_scatter | solution.py:136
  146.6 252.9 %all-gather.16.cloned.1.call-start = ((), (), s32[]{:S(2)}) async-start(), calls=%async_computation.25 | async-start | bytes 8601600 | tf_op jit(solution)/shard_map/all_gather | solution.py:127
  349.7 73.9 %reduce-scatter.28.cloned.1.call-start = ((), (), s32[]{:S(2)}) async-start(), calls=%async_computation.26 | async-start | bytes 884736 | tf_op jit(solution)/shard_map/reduce_scatter | solution.py:150
  408.1 74.0 %reduce-scatter.30.cloned.1.call-start = ((), (), s32[]{:S(2)}) async-start(), calls=%async_computation.27 | async-start | bytes 3932160 | tf_op jit(solution)/shard_map/reduce_scatter | solution.py:136
  444.1 61.3 %all-gather.18.cloned.1.call-start = ((), (), s32[]{:S(2)}) async-start(), calls=%async_computation.28 | async-start | bytes 1474560 | tf_op jit(solution)/shard_map/all_gather | solution.py:127
  487.8 42.3 %reduce-scatter.32.cloned.1.call-start = ((), (), s32[]{:S(2)}) async-start(), calls=%async_computation.29 | async-start | bytes 884736 | tf_op jit(solution)/shard_map/reduce_scatter | solution.py:150
  508.5 85.3 %reduce-scatter.38.cloned.1.call-start = ((), (), s32[]{:S(2)}) async-start(), calls=%async_computation.33 | async-start | bytes 8601600 | tf_op jit(solution)/shard_map/reduce_scatter | solution.py:169
  530.1 264.0 %reduce-scatter.34.cloned.1.call-start = ((), (), s32[]{:S(2)}) async-start(), calls=%async_computation.30 | async-start | bytes 34406400 | tf_op jit(solution)/shard_map/reduce_scatter | solution.py:136
  568.4 322.0 %all-gather.22.cloned.1.call-start = ((), (), s32[]{:S(2)}) async-start(), calls=%async_computation.34 | async-start | bytes 17203200 | tf_op jit(solution)/shard_map/all_gather | solution.py:180
  801.4 117.7 %reduce-scatter.40.cloned.1.call-start = ((), (), s32[]{:S(2)}) async-start(), calls=%async_computation.35 | async-start | bytes 884736 | tf_op jit(solution)/shard_map/reduce_scatter | solution.py:189
  903.6 65.3 %reduce-scatter.42.cloned.1.call-start = ((), (), s32[]{:S(2)}) async-start(), calls=%async_computation.36 | async-start | bytes 1474560 | tf_op jit(solution)/shard_map/reduce_scatter | solution.py:169
  943.3 50.7 %all-gather.24.cloned.1.call-start = ((), (), s32[]{:S(2)}) async-start(), calls=%async_computation.37 | async-start | bytes 1966080 | tf_op jit(solution)/shard_map/all_gather | solution.py:180
  974.1 71.5 %all-gather.20.cloned.1.call-start = ((), (), s32[]{:S(2)}) async-start(), calls=%async_computation.31 | async-start | bytes 8601600 | tf_op jit(solution)/shard_map/all_gather | solution.py:127
  974.7 89.0 %reduce-scatter.44.cloned.1.call-start = ((), (), s32[]{:S(2)}) async-start(), calls=%async_computation.38 | async-start | bytes 884736 | tf_op jit(solution)/shard_map/reduce_scatter | solution.py:189
  997.5 84.3 %reduce-scatter.36.cloned.1.call-start = ((), (), s32[]{:S(2)}) async-start(), calls=%async_computation.32 | async-start | bytes 884736 | tf_op jit(solution)/shard_map/reduce_scatter | solution.py:150
  1054.2 110.8 %reduce-scatter.46.cloned.1.call-start = ((), (), s32[]{:S(2)}) async-start(), calls=%async_computation.39 | async-start | bytes 8601600 | tf_op jit(solution)/shard_map/reduce_scatter | solution.py:169
  1101.9 158.3 %all-gather.26.cloned.1.call-start = ((), (), s32[]{:S(2)}) async-start(), calls=%async_computation.40 | async-start | bytes 17203200 | tf_op jit(solution)/shard_map/all_gather | solution.py:180
  1171.3 117.6 %copy-start.56 = (f32[384]{0:T(512)S(1)}, f32[384]{0:T(512)}, u32[]{:S(2)}) copy-start(f32[384]{0:T(512)} %copy-done.55) | copy-start | bytes 4612
  1171.3 117.6 %copy-start.58 = (f32[384]{0:T(512)S(1)}, f32[384]{0:T(512)}, u32[]{:S(2)}) copy-start(f32[384]{0:T(512)} %copy-done.57) | copy-start | bytes 4612
  1171.3 125.7 %copy-start.73 = (f32[384]{0:T(512)S(1)}, f32[384]{0:T(512)}, u32[]{:S(2)}) copy-start(f32[384]{0:T(512)} %copy-done.72) | copy-start | bytes 4612
  1171.3 117.5 %reduce-scatter.48.cloned.1.call-start = ((), (), s32[]{:S(2)}) async-start(), calls=%async_computation.41 | async-start | bytes 884736 | tf_op jit(solution)/shard_map/reduce_scatter | solution.py:189
  1273.4 63.1 %reduce-scatter.50.cloned.1.call-start = ((), (), s32[]{:S(2)}) async-start(), calls=%async_computation.42 | async-start | bytes 1474560 | tf_op jit(solution)/shard_map/reduce_scatter | solution.py:169
  1310.7 71.6 %all-gather.28.cloned.1.call-start = ((), (), s32[]{:S(2)}) async-start(), calls=%async_computation.43 | async-start | bytes 1966080 | tf_op jit(solution)/shard_map/all_gather | solution.py:180
  1341.4 142.9 %reduce-scatter.62.cloned.1.call-start = ((), (), s32[]{:S(2)}) async-start(), calls=%async_computation.53 | async-start | bytes 8601600 | tf_op jit(solution)/shard_map/reduce_scatter | solution.py:219
  1359.0 158.1 %reduce-scatter.56.cloned.1.call-start = ((), (), s32[]{:S(2)}) async-start(), calls=%async_computation.47 | async-start | bytes 1474560 | tf_op jit(solution)/shard_map/reduce_scatter | solution.py:210
  1365.5 188.4 %reduce-scatter.54.cloned.1.call-start = ((), (), s32[]{:S(2)}) async-start(), calls=%async_computation.45 | async-start | bytes 1966080 | tf_op jit(solution)/shard_map/reduce_scatter | solution.py:207
  1386.0 289.8 %reduce-scatter.58.cloned.1.call-start = ((), (), s32[]{:S(2)}) async-start(), calls=%async_computation.49 | async-start | bytes 8601600 | tf_op jit(solution)/shard_map/reduce_scatter | solution.py:213
  1404.0 395.6 %reduce-scatter.60.cloned.1.call-start = ((), (), s32[]{:S(2)}) async-start(), calls=%async_computation.51 | async-start | bytes 8601600 | tf_op jit(solution)/shard_map/reduce_scatter | solution.py:216
  1410.6 516.1 %all-gather.38.cloned.1.call-start = ((), (), s32[]{:S(2)}) async-start(), calls=%async_computation.54 | async-start | bytes 8601600 | tf_op jit(solution)/shard_map/all_gather | solution.py:236
  1484.3 472.3 %all-gather.32.cloned.1.call-start = ((), (), s32[]{:S(2)}) async-start(), calls=%async_computation.48 | async-start | bytes 1474560 | tf_op jit(solution)/shard_map/all_gather | solution.py:227
  1517.1 282.5 %copy-start.79 = (f32[384]{0:T(512)S(1)}, f32[384]{0:T(512)}, u32[]{:S(2)}) copy-start(f32[384]{0:T(512)} %get-tuple-element.10) | copy-start | bytes 4612
  1517.1 282.5 %copy-start.5 = (f32[1,192,1,6,128]{4,1,3,2,0:T(8,128)S(1)}, f32[1,192,1,6,128]{4,1,3,2,0:T(8,128)}, u32[]{:S(2)}) copy-start(f32[1,192,1,6,128]{4,1,3,2,0:T(8,128)} %copy-done.4) | copy-start | bytes 1769476
  1517.1 282.5 %copy-start.29 = (f32[1,192,1,1,128]{4,1,3,2,0:T(8,128)S(1)}, f32[1,192,1,1,128]{4,1,3,2,0:T(8,128)}, u32[]{:S(2)}) copy-start(f32[1,192,1,1,128]{4,1,3,2,0:T(8,128)} %copy-done.28) | copy-start | bytes 294916
  1517.1 282.5 %copy-start.33 = (f32[1,192,1,1,128]{4,1,3,2,0:T(8,128)S(1)}, f32[1,192,1,1,128]{4,1,3,2,0:T(8,128)}, u32[]{:S(2)}) copy-start(f32[1,192,1,1,128]{4,1,3,2,0:T(8,128)} %copy-done.32) | copy-start | bytes 294916
  1517.2 456.9 %reduce-scatter.52.cloned.1.call-start = ((), (), s32[]{:S(2)}) async-start(), calls=%async_computation.44 | async-start | bytes 884736 | tf_op jit(solution)/shard_map/reduce_scatter | solution.py:189
  1520.7 279.1 %copy-start.80 = (f32[384]{0:T(512)S(1)}, f32[384]{0:T(512)}, u32[]{:S(2)}) copy-start(f32[384]{0:T(512)} %get-tuple-element.14) | copy-start | bytes 4612
  1520.7 506.7 %all-gather.30.cloned.1.call-start = ((), (), s32[]{:S(2)}) async-start(), calls=%async_computation.46 | async-start | bytes 1966080 | tf_op jit(solution)/shard_map/all_gather | solution.py:224
  1553.9 585.1 %all-gather.34.cloned.1.call-start = ((), (), s32[]{:S(2)}) async-start(), calls=%async_computation.50 | async-start | bytes 8601600 | tf_op jit(solution)/shard_map/all_gather | solution.py:230
  1675.9 587.9 %all-gather.36.cloned.1.call-start = ((), (), s32[]{:S(2)}) async-start(), calls=%async_computation.52 | async-start | bytes 8601600 | tf_op jit(solution)/shard_map/all_gather | solution.py:233
  1799.8 136.0 %copy-start.81 = (f32[384]{0:T(512)S(1)}, f32[384]{0:T(512)}, u32[]{:S(2)}) copy-start(f32[384]{0:T(512)} %get-tuple-element.12) | copy-start | bytes 4612
  1799.8 136.0 %copy-start.31 = (f32[1,192,1,1,128]{4,1,3,2,0:T(8,128)S(1)}, f32[1,192,1,1,128]{4,1,3,2,0:T(8,128)}, u32[]{:S(2)}) copy-start(f32[1,192,1,1,128]{4,1,3,2,0:T(8,128)} %copy-done.30) | copy-start | bytes 294916
  1799.8 136.0 %copy-start.35 = (f32[1,192,1,1,128]{4,1,3,2,0:T(8,128)S(1)}, f32[1,192,1,1,128]{4,1,3,2,0:T(8,128)}, u32[]{:S(2)}) copy-start(f32[1,192,1,1,128]{4,1,3,2,0:T(8,128)} %copy-done.34) | copy-start | bytes 294916
  (72 other events, 1409.4 us)
Sparse Core Ops, SparseCore 0:
  31.5 39.2 reduce-scatter.21
  76.6 17.4 all-gather.13
  97.1 15.3 reduce-scatter.23
  146.7 197.7 reduce-scatter.25
  349.8 49.6 all-gather.15
  408.2 15.3 reduce-scatter.27
  444.2 37.9 reduce-scatter.29
  488.0 17.4 all-gather.17
  508.6 17.3 reduce-scatter.31
  530.2 63.5 reduce-scatter.37
  596.4 197.6 reduce-scatter.33
  801.6 88.7 all-gather.21
  903.8 15.3 reduce-scatter.39
  943.4 25.5 reduce-scatter.41
  974.3 19.6 all-gather.23
  995.9 49.6 all-gather.19
  1048.3 15.3 reduce-scatter.43
  1066.4 15.3 reduce-scatter.35
  1102.0 62.8 reduce-scatter.45
  1171.4 88.7 all-gather.25
  1273.5 15.3 reduce-scatter.47
  1310.8 25.5 reduce-scatter.49
  1341.5 19.6 all-gather.27
  1363.9 120.3 reduce-scatter.61
  1487.2 29.8 reduce-scatter.55
  1519.8 34.0 reduce-scatter.53
  1556.6 119.1 reduce-scatter.57
  1678.7 120.8 reduce-scatter.59
  1801.2 125.4 all-gather.37
  1928.1 28.4 all-gather.31
  1959.4 14.5 reduce-scatter.51
  1975.6 38.0 all-gather.29
  2015.1 123.8 all-gather.33
  2140.5 123.1 all-gather.35
where the time goes:
time: 2290 us; the launch traced here: 2280 us
  waiting for transfers between devices  1780 us (78%)
  blocking collectives  171 us (7%)
  matrix products  170 us (7%)
  other arithmetic  102 us (4%)
  local copies, waits for them, and re-layouts  34.1 us (1%)
    reduce_scatter x4, waiting for transfers between devices, widen(): lax.psum_scatter(partial_term(jnp.int32(0), lax.axis_size('rows') * per_d...  474 us
    all_gather x4, waiting for transfers between devices, back_widen(): gathered = lax.all_gather(grad_round, 'rows', axis=0, tiled=True)  197 us
    reduce_scatter x4, waiting for transfers between devices, back_narrow(): lax.psum_scatter(partial_term(jnp.int32(0), per_device * lax.axis_size('r...  139 us
    all_gather x4, waiting for transfers between devices, gather_rows(): return lax.all_gather(values, 'rows', axis=0, tiled=True)  132 us
    all_gather x1, waiting for transfers between devices, spread(): lax.all_gather(summed[4].astype(jnp.bfloat16), 'dp', axis=1, tiled=True)  127 us
    reduce_scatter x1, waiting for transfers between devices, spread(): lax.psum_scatter(fourth_grad.astype(jnp.bfloat16), 'dp', scatter_dimensio...  123 us
    reduce_scatter x1, waiting for transfers between devices, spread(): lax.psum_scatter(third_grad.astype(jnp.bfloat16), 'dp', scatter_dimension...  122 us
    all_gather x1, waiting for transfers between devices, spread(): lax.all_gather(summed[3].astype(jnp.bfloat16), 'dp', axis=1, tiled=True)  115 us
  transfers between devices with their start and end apart: 34, of which 31 were waited for; matrix products, arithmetic and copies ran while one was open for 7% of the time, Pallas kernels for 0%

commit v1 on v0

--- a/solution.py
+++ b/solution.py
@@ -15,6 +15,28 @@
 masked = -1e30
 
 
+def in_order(blocks, dim):
+    dims = list(blocks.shape[1:])
+    dims[dim] *= blocks.shape[0]
+    return jnp.moveaxis(blocks, 0, dim).reshape(dims)
+
+
+def grow_blocks(array, axis):
+    devices = lax.axis_size(axis)
+    pieces = array[None]
+    for level in range(devices.bit_length() - 1):
+        bit = 1 << level
+        partner_block = lax.ppermute(pieces, axis, [(i, i ^ bit) for i in range(devices)])
+        both = jnp.stack([pieces, partner_block])
+        upper = lax.axis_index(axis) >> level & 1
+        pieces = jnp.where(upper == 0, both, both[::-1]).reshape(-1, *array.shape)
+    return pieces
+
+
+def doubled_up(x, axis, dim):
+    return in_order(grow_blocks(x, axis), dim)
+
+
 def rotate_half(values):
     half_dim = values.shape[-1] // 2
     return jnp.concatenate([-values[..., half_dim:], values[..., :half_dim]], axis=-1)
@@ -227,9 +249,7 @@
         lax.all_gather(summed[1].astype(jnp.bfloat16), "dp", axis=1, tiled=True).astype(
             jnp.float32
         ),
-        lax.all_gather(summed[2].astype(jnp.bfloat16), "dp", axis=1, tiled=True).astype(
-            jnp.float32
-        ),
+        doubled_up(summed[2].astype(jnp.bfloat16), "dp", 1).astype(jnp.float32),
         lax.all_gather(summed[3].astype(jnp.bfloat16), "dp", axis=1, tiled=True).astype(
             jnp.float32
         ),

time: 2290 us -> 2320 us (1.013)
    all_gather x1, waiting for transfers between devices: 127 us -> 241 us  [spread(): lax.all_gather(summed[4].astype(jnp.bfloat16), 'dp', axis=1, tiled=True)]
    all_gather x1 -> x0, waiting for transfers between devices: 108 us -> none  [spread(): lax.all_gather(summed[2].astype(jnp.bfloat16), 'dp', axis=1, tiled=True)]
    all_gather x1, waiting for transfers between devices: 115 us -> 77 us  [spread(): lax.all_gather(summed[3].astype(jnp.bfloat16), 'dp', axis=1, tiled=True)]
    reduce_scatter x1, waiting for transfers between devices: 123 us -> 150 us  [spread(): lax.psum_scatter(fourth_grad.astype(jnp.bfloat16), 'dp', scatter_dimensio...]
  transfers between devices with their start and end apart: 34 -> 35, of which waited for: 31 -> 30; matrix products, arithmetic and copies ran while one was open for 7% -> 8% of each run, Pallas kernels for 0% -> 0%
where the time goes in v1:
time: 2320 us
  waiting for transfers between devices  1790 us (77%)
  blocking collectives  171 us (7%)
  matrix products  170 us (7%)
  other arithmetic  118 us (5%)
  local copies, waits for them, and re-layouts  45.2 us (2%)
    reduce_scatter x4, waiting for transfers between devices, widen(): lax.psum_scatter(partial_term(jnp.int32(0), lax.axis_size('rows') * per_d...  474 us
    all_gather x1, waiting for transfers between devices, spread(): lax.all_gather(summed[4].astype(jnp.bfloat16), 'dp', axis=1, tiled=True)  241 us
    all_gather x4, waiting for transfers between devices, back_widen(): gathered = lax.all_gather(grad_round, 'rows', axis=0, tiled=True)  197 us
    reduce_scatter x1, waiting for transfers between devices, spread(): lax.psum_scatter(fourth_grad.astype(jnp.bfloat16), 'dp', scatter_dimensio...  150 us
    reduce_scatter x4, waiting for transfers between devices, back_narrow(): lax.psum_scatter(partial_term(jnp.int32(0), per_device * lax.axis_size('r...  139 us
    all_gather x4, waiting for transfers between devices, gather_rows(): return lax.all_gather(values, 'rows', axis=0, tiled=True)  132 us
    reduce_scatter x1, waiting for transfers between devices, spread(): lax.psum_scatter(third_grad.astype(jnp.bfloat16), 'dp', scatter_dimension...  122 us
    all_gather x1, waiting for transfers between devices, spread(): lax.all_gather(summed[3].astype(jnp.bfloat16), 'dp', axis=1, tiled=True)  77 us
  transfers between devices with their start and end apart: 35, of which 30 were waited for; matrix products, arithmetic and copies ran while one was open for 8% of the time, Pallas kernels for 0%

profile of v1, /device:TPU:0, one launch (start us, length us, event | category | flops | bytes accessed | tf_op | source)
XLA Modules:
  0.0 2315.1 jit_solution(5945569344935593002)
XLA Ops:
  32.6 38.2 %reduce-scatter.22.cloned.1.call-done = f32[192,1024]{1,0:T(8,128)} async-done(((f32[768,1024]{1,0:T(8,128)}), f32[192,1024]{1,0:T(8,128)}) %reduce-scatter.22.cloned.1.call-update) | async-done | bytes 786448 | tf_op jit(solution)/shard_map/reduce_scatter | solution.py:158
  77.2 16.9 all-gather.13.cloned.1.call-done
  97.0 10.2 slice_bitcast_fusion.4
  121.1 8.7 all_gather.62
  130.7 15.9 fusion.5
  146.7 197.8 %reduce-scatter.26.cloned.1.call-done = f32[192,8960]{1,0:T(8,128)} async-done(((f32[768,8960]{1,0:T(8,128)}), f32[192,8960]{1,0:T(8,128)}) %reduce-scatter.26.cloned.1.call-update) | async-done | bytes 6881296 | tf_op jit(solution)/shard_map/reduce_scatter | solution.py:158
  350.2 49.3 %all-gather.15.cloned.1.call-done = bf16[768,4480]{1,0:T(8,128)(2,1)} async-done(((bf16[192,4480]{1,0:T(8,128)(2,1)}), bf16[768,4480]{1,0:T(8,128)(2,1)}) %all-gather.15.cloned.1.call-update) | async-done | bytes 6881296 | tf_op jit(solution)/shard_map/all_gather | solution.py:149
  399.5 8.5 fusion.30
  408.1 15.5 reduce-scatter.28.cloned.1.call-done
  431.3 8.7 all_gather.64
  444.1 38.0 %reduce-scatter.30.cloned.1.call-done = f32[192,1024]{1,0:T(8,128)} async-done(((f32[768,1024]{1,0:T(8,128)}), f32[192,1024]{1,0:T(8,128)}) %reduce-scatter.30.cloned.1.call-update) | async-done | bytes 786448 | tf_op jit(solution)/shard_map/reduce_scatter | solution.py:158
  487.9 17.5 all-gather.17.cloned.1.call-done
  508.5 13.0 all_gather.68
  540.2 10.2 all_gather.66
  551.2 17.1 fusion.3
  568.4 25.3 %reduce-scatter.38.cloned.1.call-done = bf16[192,4480]{1,0:T(8,128)(2,1)} async-done(((bf16[768,4480]{1,0:T(8,128)(2,1)}), bf16[192,4480]{1,0:T(8,128)(2,1)}) %reduce-scatter.38.cloned.1.call-update) | async-done | bytes 1720336 | tf_op jit(solution)/shard_map/reduce_scatter | solution.py:191
  593.7 200.3 %reduce-scatter.34.cloned.1.call-done = f32[192,8960]{1,0:T(8,128)} async-done(((f32[768,8960]{1,0:T(8,128)}), f32[192,8960]{1,0:T(8,128)}) %reduce-scatter.34.cloned.1.call-update) | async-done | bytes 6881296 | tf_op jit(solution)/shard_map/reduce_scatter | solution.py:158
  801.5 88.9 %all-gather.21.cloned.1.call-done = bf16[768,8960]{1,0:T(8,128)(2,1)} async-done(((bf16[192,8960]{1,0:T(8,128)(2,1)}), bf16[768,8960]{1,0:T(8,128)(2,1)}) %all-gather.21.cloned.1.call-update) | async-done | bytes 13762576 | tf_op jit(solution)/shard_map/all_gather | solution.py:202
  890.4 13.2 fusion.37
  903.7 15.5 reduce-scatter.40.cloned.1.call-done
  930.8 8.7 all_gather.70
  943.3 25.7 %reduce-scatter.42.cloned.1.call-done = bf16[192,768]{1,0:T(8,128)(2,1)} async-done(((bf16[768,768]{1,0:T(8,128)(2,1)}), bf16[192,768]{1,0:T(8,128)(2,1)}) %reduce-scatter.42.cloned.1.call-update) | async-done | bytes 294928 | tf_op jit(solution)/shard_map/reduce_scatter | solution.py:191
  974.8 19.2 all-gather.23.cloned.1.call-done
  997.7 47.9 %all-gather.19.cloned.1.call-done = bf16[768,4480]{1,0:T(8,128)(2,1)} async-done(((bf16[192,4480]{1,0:T(8,128)(2,1)}), bf16[768,4480]{1,0:T(8,128)(2,1)}) %all-gather.19.cloned.1.call-update) | async-done | bytes 6881296 | tf_op jit(solution)/shard_map/all_gather | solution.py:149
  1054.2 9.5 reduce-scatter.44.cloned.1.call-done
  1072.5 9.3 reduce-scatter.36.cloned.1.call-done
  1084.1 9.2 all_gather.72
  1102.0 63.0 %reduce-scatter.46.cloned.1.call-done = bf16[192,4480]{1,0:T(8,128)(2,1)} async-done(((bf16[768,4480]{1,0:T(8,128)(2,1)}), bf16[192,4480]{1,0:T(8,128)(2,1)}) %reduce-scatter.46.cloned.1.call-update) | async-done | bytes 1720336 | tf_op jit(solution)/shard_map/reduce_scatter | solution.py:191
  1171.4 88.9 %all-gather.25.cloned.1.call-done = bf16[768,8960]{1,0:T(8,128)(2,1)} async-done(((bf16[192,8960]{1,0:T(8,128)(2,1)}), bf16[768,8960]{1,0:T(8,128)(2,1)}) %all-gather.25.cloned.1.call-update) | async-done | bytes 13762576 | tf_op jit(solution)/shard_map/all_gather | solution.py:202
  1260.2 13.1 fusion.36
  1273.4 15.4 reduce-scatter.48.cloned.1.call-done
  1298.2 8.7 all_gather.74
  1311.1 25.3 %reduce-scatter.50.cloned.1.call-done = bf16[192,768]{1,0:T(8,128)(2,1)} async-done(((bf16[768,768]{1,0:T(8,128)(2,1)}), bf16[192,768]{1,0:T(8,128)(2,1)}) %reduce-scatter.50.cloned.1.call-update) | async-done | bytes 294928 | tf_op jit(solution)/shard_map/reduce_scatter | solution.py:191
  1365.6 11.7 convolution_convert_fusion
  1386.1 11.1 convolution_convert_fusion.1
  1410.7 73.6 %reduce-scatter.62.cloned.1.call-done = bf16[2,1120,384]{2,1,0:T(8,128)(2,1)} async-done(((bf16[2,4480,384]{2,1,0:T(8,128)(2,1)}), bf16[2,1120,384]{2,1,0:T(8,128)(2,1)}) %reduce-scatter.62.cloned.1.call-update) | async-done | bytes 1720336 | tf_op jit(solution)/shard_map/reduce_scatter | solution.py:241
  1484.4 32.7 %reduce-scatter.56.cloned.1.call-done = bf16[2,192,384]{2,1,0:T(8,128)(2,1)} async-done(((bf16[2,768,384]{2,1,0:T(8,128)(2,1)}), bf16[2,192,384]{2,1,0:T(8,128)(2,1)}) %reduce-scatter.56.cloned.1.call-update) | async-done | bytes 294928 | tf_op jit(solution)/shard_map/reduce_scatter | solution.py:232
  1520.7 33.2 %reduce-scatter.54.cloned.1.call-done = bf16[2,96,1024]{2,1,0:T(8,128)(2,1)} async-done(((bf16[2,384,1024]{2,1,0:T(8,128)(2,1)}), bf16[2,96,1024]{2,1,0:T(8,128)(2,1)}) %reduce-scatter.54.cloned.1.call-update) | async-done | bytes 393232 | tf_op jit(solution)/shard_map/reduce_scatter | solution.py:229
  1554.2 121.7 %reduce-scatter.58.cloned.1.call-done = bf16[2,96,4480]{2,1,0:T(8,128)(2,1)} async-done(((bf16[2,384,4480]{2,1,0:T(8,128)(2,1)}), bf16[2,96,4480]{2,1,0:T(8,128)(2,1)}) %reduce-scatter.58.cloned.1.call-update) | async-done | bytes 1720336 | tf_op jit(solution)/shard_map/reduce_scatter | solution.py:235
  1677.3 150.3 %reduce-scatter.60.cloned.1.call-done = bf16[2,96,4480]{2,1,0:T(8,128)(2,1)} async-done(((bf16[2,384,4480]{2,1,0:T(8,128)(2,1)}), bf16[2,96,4480]{2,1,0:T(8,128)(2,1)}) %reduce-scatter.60.cloned.1.call-update) | async-done | bytes 1720336 | tf_op jit(solution)/shard_map/reduce_scatter | solution.py:238
  1837.1 241.2 %all-gather.35.cloned.1.call-done = bf16[2,4480,384]{2,1,0:T(8,128)(2,1)} async-done(((bf16[2,1120,384]{2,1,0:T(8,128)(2,1)}), bf16[2,4480,384]{2,1,0:T(8,128)(2,1)}) %all-gather.35.cloned.1.call-update) | async-done | bytes 6881296 | tf_op jit(solution)/shard_map/all_gather | solution.py:256
  2078.4 9.0 convert_element_type.315
  2087.6 28.0 %all-gather.31.cloned.1.call-done = bf16[2,768,384]{2,1,0:T(8,128)(2,1)} async-done(((bf16[2,192,384]{2,1,0:T(8,128)(2,1)}), bf16[2,768,384]{2,1,0:T(8,128)(2,1)}) %all-gather.31.cloned.1.call-update) | async-done | bytes 1179664 | tf_op jit(solution)/shard_map/all_gather | solution.py:249
  2118.5 15.7 reduce-scatter.52.cloned.1.call-done
  2141.8 41.7 %all-reduce = (f32[2,1536]{1,0:T(2,128)S(1)}, f32[2,2048]{1,0:T(2,128)S(1)}, f32[2,1536]{1,0:T(2,128)S(1)}) all-reduce(f32[2,1536]{1,0:T(2,128)S(1)} %maximum_dynamic-update-slice_fusion.1, f32[2,2048]{1,0:T(2,128)S(1)} %maximum_dynamic-update-slice_fusion, ...), channel_id=1, replica_groups=mesh['dp'=4,'rows'=4,'cols'=2] {'dp','rows','cols'}, use_global_device_ids=true, to_apply=%region_40.41 | all-reduce | flops 10240 | bytes 81920 | tf_op jit(solution)/shard_map/psum | solution.py:353
  2210.9 11.1 copy.61
  2222.0 77.0 %all-gather.33.cloned.1.call-done = bf16[2,384,4480]{2,1,0:T(8,128)(2,1)} async-done(((bf16[2,96,4480]{2,1,0:T(8,128)(2,1)}), bf16[2,384,4480]{2,1,0:T(8,128)(2,1)}) %all-gather.33.cloned.1.call-update) | async-done | bytes 6881296 | tf_op jit(solution)/shard_map/all_gather | solution.py:253
  2299.0 9.0 convert_element_type.314
  (395 shorter events, 279.0 us)
Async XLA Ops:
  7.2 63.6 %reduce-scatter.22.cloned.1.call-start = ((), (), s32[]{:S(2)}) async-start(), calls=%async_computation.21 | async-start | bytes 3932160 | tf_op jit(solution)/shard_map/reduce_scatter | solution.py:158
  8.0 423.2 %copy-start.64 = (f32[384]{0:T(512)}, f32[384]{0:T(512)S(1)}, u32[]{:S(2)}) copy-start(f32[384]{0:T(512)S(1)} %get-tuple-element.18) | copy-start | bytes 4612
  31.4 62.7 %all-gather.13.cloned.1.call-start = ((), (), s32[]{:S(2)}) async-start(), calls=%async_computation.22 | async-start | bytes 1474560 | tf_op jit(solution)/shard_map/all_gather | solution.py:149
  32.6 452.2 %copy-start.16 = (f32[192,128]{1,0:T(8,128)}, f32[192,128]{1,0:T(8,128)S(1)}, u32[]{:S(2)}) copy-start(f32[192,128]{1,0:T(8,128)S(1)} %get-tuple-element.61) | copy-start | bytes 294916
  32.6 452.2 %copy-start.19 = (f32[192,128]{1,0:T(8,128)}, f32[192,128]{1,0:T(8,128)S(1)}, u32[]{:S(2)}) copy-start(f32[192,128]{1,0:T(8,128)S(1)} %get-tuple-element.62) | copy-start | bytes 294916
  76.5 36.0 %reduce-scatter.24.cloned.1.call-start = ((), (), s32[]{:S(2)}) async-start(), calls=%async_computation.23 | async-start | bytes 884736 | tf_op jit(solution)/shard_map/reduce_scatter | solution.py:172
  97.0 247.5 %reduce-scatter.26.cloned.1.call-start = ((), (), s32[]{:S(2)}) async-start(), calls=%async_computation.24 | async-start | bytes 34406400 | tf_op jit(solution)/shard_map/reduce_scatter | solution.py:158
  146.6 252.9 %all-gather.15.cloned.1.call-start = ((), (), s32[]{:S(2)}) async-start(), calls=%async_computation.25 | async-start | bytes 8601600 | tf_op jit(solution)/shard_map/all_gather | solution.py:149
  349.7 73.9 %reduce-scatter.28.cloned.1.call-start = ((), (), s32[]{:S(2)}) async-start(), calls=%async_computation.26 | async-start | bytes 884736 | tf_op jit(solution)/shard_map/reduce_scatter | solution.py:172
  408.1 74.0 %reduce-scatter.30.cloned.1.call-start = ((), (), s32[]{:S(2)}) async-start(), calls=%async_computation.27 | async-start | bytes 3932160 | tf_op jit(solution)/shard_map/reduce_scatter | solution.py:158
  444.1 61.3 %all-gather.17.cloned.1.call-start = ((), (), s32[]{:S(2)}) async-start(), calls=%async_computation.28 | async-start | bytes 1474560 | tf_op jit(solution)/shard_map/all_gather | solution.py:149
  487.8 42.3 %reduce-scatter.32.cloned.1.call-start = ((), (), s32[]{:S(2)}) async-start(), calls=%async_computation.29 | async-start | bytes 884736 | tf_op jit(solution)/shard_map/reduce_scatter | solution.py:172
  508.5 85.3 %reduce-scatter.38.cloned.1.call-start = ((), (), s32[]{:S(2)}) async-start(), calls=%async_computation.33 | async-start | bytes 8601600 | tf_op jit(solution)/shard_map/reduce_scatter | solution.py:191
  530.1 264.0 %reduce-scatter.34.cloned.1.call-start = ((), (), s32[]{:S(2)}) async-start(), calls=%async_computation.30 | async-start | bytes 34406400 | tf_op jit(solution)/shard_map/reduce_scatter | solution.py:158
  568.4 322.0 %all-gather.21.cloned.1.call-start = ((), (), s32[]{:S(2)}) async-start(), calls=%async_computation.34 | async-start | bytes 17203200 | tf_op jit(solution)/shard_map/all_gather | solution.py:202
  801.4 117.7 %reduce-scatter.40.cloned.1.call-start = ((), (), s32[]{:S(2)}) async-start(), calls=%async_computation.35 | async-start | bytes 884736 | tf_op jit(solution)/shard_map/reduce_scatter | solution.py:211
  903.6 65.3 %reduce-scatter.42.cloned.1.call-start = ((), (), s32[]{:S(2)}) async-start(), calls=%async_computation.36 | async-start | bytes 1474560 | tf_op jit(solution)/shard_map/reduce_scatter | solution.py:191
  943.3 50.7 %all-gather.23.cloned.1.call-start = ((), (), s32[]{:S(2)}) async-start(), calls=%async_computation.37 | async-start | bytes 1966080 | tf_op jit(solution)/shard_map/all_gather | solution.py:202
  974.1 71.5 %all-gather.19.cloned.1.call-start = ((), (), s32[]{:S(2)}) async-start(), calls=%async_computation.31 | async-start | bytes 8601600 | tf_op jit(solution)/shard_map/all_gather | solution.py:149
  974.7 89.0 %reduce-scatter.44.cloned.1.call-start = ((), (), s32[]{:S(2)}) async-start(), calls=%async_computation.38 | async-start | bytes 884736 | tf_op jit(solution)/shard_map/reduce_scatter | solution.py:211
  997.4 84.4 %copy-start.3 = (bf16[384,384]{1,0:T(8,128)(2,1)S(1)}, bf16[384,384]{1,0:T(8,128)(2,1)}, u32[]{:S(2)}) copy-start(bf16[384,384]{1,0:T(8,128)(2,1)} %reduce-scatter.32.cloned.1.call-done) | copy-start | bytes 884740
  997.5 84.3 %reduce-scatter.36.cloned.1.call-start = ((), (), s32[]{:S(2)}) async-start(), calls=%async_computation.32 | async-start | bytes 884736 | tf_op jit(solution)/shard_map/reduce_scatter | solution.py:172
  1054.2 110.8 %reduce-scatter.46.cloned.1.call-start = ((), (), s32[]{:S(2)}) async-start(), calls=%async_computation.39 | async-start | bytes 8601600 | tf_op jit(solution)/shard_map/reduce_scatter | solution.py:191
  1101.9 158.3 %all-gather.25.cloned.1.call-start = ((), (), s32[]{:S(2)}) async-start(), calls=%async_computation.40 | async-start | bytes 17203200 | tf_op jit(solution)/shard_map/all_gather | solution.py:202
  1171.3 117.6 %copy-start.56 = (f32[384]{0:T(512)S(1)}, f32[384]{0:T(512)}, u32[]{:S(2)}) copy-start(f32[384]{0:T(512)} %copy-done.55) | copy-start | bytes 4612
  1171.3 117.6 %copy-start.58 = (f32[384]{0:T(512)S(1)}, f32[384]{0:T(512)}, u32[]{:S(2)}) copy-start(f32[384]{0:T(512)} %copy-done.57) | copy-start | bytes 4612
  1171.3 125.7 %copy-start.73 = (f32[384]{0:T(512)S(1)}, f32[384]{0:T(512)}, u32[]{:S(2)}) copy-start(f32[384]{0:T(512)} %copy-done.72) | copy-start | bytes 4612
  1171.3 117.5 %reduce-scatter.48.cloned.1.call-start = ((), (), s32[]{:S(2)}) async-start(), calls=%async_computation.41 | async-start | bytes 884736 | tf_op jit(solution)/shard_map/reduce_scatter | solution.py:211
  1273.4 63.1 %reduce-scatter.50.cloned.1.call-start = ((), (), s32[]{:S(2)}) async-start(), calls=%async_computation.42 | async-start | bytes 1474560 | tf_op jit(solution)/shard_map/reduce_scatter | solution.py:191
  1310.7 71.6 %all-gather.27.cloned.1.call-start = ((), (), s32[]{:S(2)}) async-start(), calls=%async_computation.43 | async-start | bytes 1966080 | tf_op jit(solution)/shard_map/all_gather | solution.py:202
  1341.4 142.9 %reduce-scatter.62.cloned.1.call-start = ((), (), s32[]{:S(2)}) async-start(), calls=%async_computation.52 | async-start | bytes 8601600 | tf_op jit(solution)/shard_map/reduce_scatter | solution.py:241
  1359.0 158.1 %reduce-scatter.56.cloned.1.call-start = ((), (), s32[]{:S(2)}) async-start(), calls=%async_computation.47 | async-start | bytes 1474560 | tf_op jit(solution)/shard_map/reduce_scatter | solution.py:232
  1365.5 188.4 %reduce-scatter.54.cloned.1.call-start = ((), (), s32[]{:S(2)}) async-start(), calls=%async_computation.45 | async-start | bytes 1966080 | tf_op jit(solution)/shard_map/reduce_scatter | solution.py:229
  1386.0 289.8 %reduce-scatter.58.cloned.1.call-start = ((), (), s32[]{:S(2)}) async-start(), calls=%async_computation.49 | async-start | bytes 8601600 | tf_op jit(solution)/shard_map/reduce_scatter | solution.py:235
  1404.0 423.7 %reduce-scatter.60.cloned.1.call-start = ((), (), s32[]{:S(2)}) async-start(), calls=%async_computation.50 | async-start | bytes 8601600 | tf_op jit(solution)/shard_map/reduce_scatter | solution.py:238
  1410.6 667.8 %all-gather.35.cloned.1.call-start = ((), (), s32[]{:S(2)}) async-start(), calls=%async_computation.53 | async-start | bytes 8601600 | tf_op jit(solution)/shard_map/all_gather | solution.py:256
  1484.3 631.3 %all-gather.31.cloned.1.call-start = ((), (), s32[]{:S(2)}) async-start(), calls=%async_computation.48 | async-start | bytes 1474560 | tf_op jit(solution)/shard_map/all_gather | solution.py:249
  1517.1 617.0 %reduce-scatter.52.cloned.1.call-start = ((), (), s32[]{:S(2)}) async-start(), calls=%async_computation.44 | async-start | bytes 884736 | tf_op jit(solution)/shard_map/reduce_scatter | solution.py:211
  1520.6 666.9 %all-gather.29.cloned.1.call-start = ((), (), s32[]{:S(2)}) async-start(), calls=%async_computation.46 | async-start | bytes 1966080 | tf_op jit(solution)/shard_map/all_gather | solution.py:246
  1553.9 745.1 %all-gather.33.cloned.1.call-start = ((), (), s32[]{:S(2)}) async-start(), calls=%async_computation.51 | async-start | bytes 8601600 | tf_op jit(solution)/shard_map/all_gather | solution.py:253
  1675.8 151.9 %collective-permute-start = (bf16[1,2,96,4480]{3,2,1,0:T(8,128)(2,1)}, bf16[1,2,96,4480]{3,2,1,0:T(8,128)(2,1)}, u32[]{:S(2)}, u32[]{:S(2)}) collective-permute-start(bf16[1,2,96,4480]{3,2,1,0:T(8,128)(2,1)} %bitcast.329), channel_id=1, source_target_pairs={{0,8},{8,0},{16,24},{24,16},{1,9},{9,1},{17,25},{25,17},{2,10},{10... | collective-permute-start | bytes 5160968 | tf_op jit(solution)/shard_map/ppermute | solution.py:29
  1833.6 357.3 %collective-permute-start.1 = (bf16[2,2,96,4480]{3,2,1,0:T(8,128)(2,1)}, bf16[2,2,96,4480]{3,2,1,0:T(8,128)(2,1)}, u32[]{:S(2)}, u32[]{:S(2)}) collective-permute-start(bf16[2,2,96,4480]{3,2,1,0:T(8,128)(2,1)} %get-tuple-element.43), channel_id=1, source_target_pairs={{0,16},{8,24},{16,0},{24,8},{1,17},{9,25},{17,1},{25,9},{2,18},{10... | collective-permute-start | bytes 10321928 | tf_op jit(solution)/shard_map/ppermute | solution.py:29
  1837.1 250.3 %copy-start.81 = (f32[384]{0:T(512)S(1)}, f32[384]{0:T(512)}, u32[]{:S(2)}) copy-start(f32[384]{0:T(512)} %get-tuple-element.12) | copy-start | bytes 4612
  1837.1 250.3 %copy-start.31 = (f32[1,192,1,1,128]{4,1,3,2,0:T(8,128)S(1)}, f32[1,192,1,1,128]{4,1,3,2,0:T(8,128)}, u32[]{:S(2)}) copy-start(f32[1,192,1,1,128]{4,1,3,2,0:T(8,128)} %copy-done.30) | copy-start | bytes 294916
  1837.1 250.3 %copy-start.35 = (f32[1,192,1,1,128]{4,1,3,2,0:T(8,128)S(1)}, f32[1,192,1,1,128]{4,1,3,2,0:T(8,128)}, u32[]{:S(2)}) copy-start(f32[1,192,1,1,128]{4,1,3,2,0:T(8,128)} %copy-done.34) | copy-start | bytes 294916
  2087.4 97.9 %copy-start.71 = (f32[384]{0:T(512)S(1)}, f32[384]{0:T(512)}, u32[]{:S(2)}) copy-start(f32[384]{0:T(512)} %copy-done.70) | copy-start | bytes 4612
  2087.4 97.9 %copy-start.11 = (bf16[384,384]{1,0:T(8,128)(2,1)S(1)}, bf16[384,384]{1,0:T(8,128)(2,1)}, u32[]{:S(2)}) copy-start(bf16[384,384]{1,0:T(8,128)(2,1)} %reduce-scatter.48.cloned.1.call-done) | copy-start | bytes 884740
  2087.4 97.9 %copy-start.77 = (f32[384]{0:T(512)S(1)}, f32[384]{0:T(512)}, u32[]{:S(2)}) copy-start(f32[384]{0:T(512)} %copy-done.76) | copy-start | bytes 4612
  (73 other events, 1108.2 us)
Sparse Core Ops, SparseCore 0:
  31.5 39.2 reduce-scatter.21
  76.6 17.4 all-gather.12
  97.1 15.3 reduce-scatter.23
  146.7 197.7 reduce-scatter.25
  349.8 49.6 all-gather.14
  408.2 15.3 reduce-scatter.27
  444.2 37.9 reduce-scatter.29
  488.0 17.4 all-gather.16
  508.6 17.3 reduce-scatter.31
  530.2 63.5 reduce-scatter.37
  596.4 197.6 reduce-scatter.33
  801.6 88.7 all-gather.20
  903.8 15.3 reduce-scatter.39
  943.4 25.5 reduce-scatter.41
  974.3 19.6 all-gather.22
  995.9 49.6 all-gather.18
  1048.3 15.3 reduce-scatter.43
  1066.4 15.3 reduce-scatter.35
  1102.0 62.8 reduce-scatter.45
  1171.4 88.7 all-gather.24
  1273.5 15.3 reduce-scatter.47
  1310.8 25.5 reduce-scatter.49
  1341.5 19.6 all-gather.26
  1363.9 120.3 reduce-scatter.61
  1487.2 29.8 reduce-scatter.55
  1519.8 34.0 reduce-scatter.53
  1556.6 119.1 reduce-scatter.57
  1678.7 148.9 reduce-scatter.59
  1829.2 249.0 all-gather.34
  2079.8 35.7 all-gather.30
  2118.5 15.5 reduce-scatter.51
  2135.7 37.9 all-gather.28
  2175.1 123.8 all-gather.32
